TPU v7x, 32 devices: a whole 2x2x4 slice. The times are simulated.
32 devices in a mesh: grp: 2 (over y), seq: 4 (over z), dp: 2 (over x), pipe: 2 (over core).
Axes of the slice: x: 2, y: 2, z: 4, core: 2. Of those that a mesh axis runs over, the one named last changes fastest.
Arguments:
- embeddings: bfloat16 [4, 512, 1664], P(('grp', 'dp'), 'seq'), parts along dimension 0, may hold values from -650 to 650
- upstream: bfloat16 [4, 512, 1664], P(('grp', 'dp'), 'seq'), parts along dimension 0, may hold values from -6 to 6
- attn_weights: bfloat16 [4, 1664, 832], P(None, ('seq', 'dp'), 'pipe'), may hold values from -1.2747549 to 1.2747549
Outputs:
- input_grads: bfloat16 [4, 512, 1664], P(('grp', 'dp'), 'seq'), parts along dimension 0
- weight_grads: float32 [8, 1664, 832], P('grp', ('seq', 'dp'), 'pipe'), parts along dimension 0
There are 2 independent parts, one for each index of `grp`. A program takes and returns all parts, laid end to end along the dimension named above; an argument that names none is the same for every part. Nothing has to cross between parts.
All inputs are finite; a program needn't handle non-finite values.
Results may differ from a plain program's by a relative error of at most 0.014.
The roundings to bfloat16 on the way count: a program that leaves them out, or rounds other values in their place, can miss the bound.
Values may be sent and summed in bfloat16 or wider, within the bound.
No kernel may reach another device: no remote copies, remote signals or barrier semaphores. Data moves between devices by JAX's collectives and lax.ppermute only.
A program may use at most 128 MiB of HBM per device.

v0:
```python
import math
import jax
import jax.numpy as jnp
from jax import lax
from jax.sharding import PartitionSpec as P

HD = 104
EPSILON = 1e-06


def local(embeddings, upstream, attn_weights):
    tokens = embeddings[0]
    row_gradients = upstream[0]
    row_count = tokens.shape[0]
    weights = lax.all_gather(attn_weights, ("seq", "dp"), axis=1, tiled=True)
    local_width = weights.shape[2]
    head_count = local_width // HD
    score_scale = HD ** (-0.5)
    features = tokens.astype(jnp.float32)
    row_mean = jnp.mean(features, axis=1, keepdims=True)
    mean_removed = features - row_mean
    variance = jnp.mean(mean_removed * mean_removed, axis=1, keepdims=True)
    inverse_deviation = lax.rsqrt(variance + EPSILON)
    standardized_input = mean_removed * inverse_deviation
    normalized_rows = standardized_input.astype(jnp.bfloat16)
    proj = jnp.einsum(
        "td,cdh->cth", normalized_rows, weights[:3], preferred_element_type=jnp.float32
    ).astype(jnp.bfloat16)
    gathered = lax.all_gather(proj[1:], "seq", axis=1, tiled=True)
    key_count = gathered.shape[1]
    query_heads = proj[0].reshape(row_count, head_count, HD).transpose(1, 0, 2)
    key_heads = gathered[0].reshape(key_count, head_count, HD).transpose(1, 0, 2)
    value_heads = gathered[1].reshape(key_count, head_count, HD).transpose(1, 0, 2)
    grad_att = jnp.dot(row_gradients, weights[3], preferred_element_type=jnp.float32).astype(
        jnp.bfloat16
    )
    grad_heads = grad_att.reshape(row_count, head_count, HD).transpose(1, 0, 2)

    def one_head(items):
        query_rows, key_rows, value_rows, grad_out = items
        scores = jnp.dot(query_rows, key_rows.T, preferred_element_type=jnp.float32) * score_scale
        row_max = jnp.max(scores, axis=1, keepdims=True)
        log_total = row_max + jnp.log(jnp.sum(jnp.exp(scores - row_max), axis=1, keepdims=True))
        probs = jnp.exp(scores - log_total).astype(jnp.bfloat16)
        attended = jnp.dot(probs, value_rows, preferred_element_type=jnp.float32).astype(
            jnp.bfloat16
        )
        row_delta = jnp.sum(
            grad_out.astype(jnp.float32) * attended.astype(jnp.float32), axis=1, keepdims=True
        )
        dprobs = jnp.dot(grad_out, value_rows.T, preferred_element_type=jnp.float32)
        dscores = (probs.astype(jnp.float32) * (dprobs - row_delta) * score_scale).astype(
            jnp.bfloat16
        )
        grad_q = jnp.dot(dscores, key_rows, preferred_element_type=jnp.float32).astype(jnp.bfloat16)
        key_term = jnp.dot(dscores.T, query_rows, preferred_element_type=jnp.float32)
        value_term = jnp.dot(probs.T, grad_out, preferred_element_type=jnp.float32)
        return (attended, grad_q, key_term, value_term)

    attended_h, grad_q_h, key_h, value_h = lax.map(
        one_head, (query_heads, key_heads, value_heads, grad_heads)
    )
    attended_flat = attended_h.transpose(1, 0, 2).reshape(row_count, local_width)
    grad_q = grad_q_h.transpose(1, 0, 2).reshape(1, row_count, local_width)
    key_terms = key_h.transpose(1, 0, 2).reshape(key_count, local_width)
    value_terms = value_h.transpose(1, 0, 2).reshape(key_count, local_width)
    both_terms = jnp.stack([key_terms, value_terms])
    owned = lax.psum_scatter(
        both_terms.astype(jnp.bfloat16), "seq", scatter_dimension=1, tiled=True
    )
    grad_qkv = jnp.concatenate([grad_q, owned], axis=0)
    token_count = row_count * lax.axis_size("seq") * lax.axis_size("dp")
    grad_factor = 1.0 / math.sqrt(token_count)
    terms_qkv = jnp.einsum(
        "td,cth->cdh", normalized_rows, grad_qkv, preferred_element_type=jnp.float32
    )
    term_out = jnp.einsum(
        "td,th->dh", row_gradients, attended_flat, preferred_element_type=jnp.float32
    )
    terms = jnp.concatenate([terms_qkv, term_out[None]], axis=0) * grad_factor
    seq_summed = lax.psum_scatter(
        terms.astype(jnp.bfloat16), "seq", scatter_dimension=1, tiled=True
    )
    weight_grads = lax.psum_scatter(seq_summed, "dp", scatter_dimension=1, tiled=True).astype(
        jnp.float32
    )
    input_part = jnp.einsum(
        "cth,cdh->td", grad_qkv, weights[:3], preferred_element_type=jnp.float32
    )
    reduced_total = lax.psum(input_part.astype(jnp.bfloat16), "pipe").astype(jnp.float32)
    leading_term = jnp.mean(reduced_total, axis=1, keepdims=True)
    trailing_term = jnp.mean(reduced_total * standardized_input, axis=1, keepdims=True)
    input_gradient = (
        row_gradients.astype(jnp.float32)
        + inverse_deviation * (reduced_total - leading_term - standardized_input * trailing_term)
    ).astype(jnp.bfloat16)
    return (input_gradient[None], weight_grads)


def solution(mesh):
    in_specs = (
        P(("grp", "dp"), "seq", None),
        P(("grp", "dp"), "seq", None),
        P(None, ("seq", "dp"), "pipe"),
    )
    out_specs = (P(("grp", "dp"), "seq", None), P("grp", ("seq", "dp"), "pipe"))
    return jax.shard_map(local, mesh=mesh, in_specs=in_specs, out_specs=out_specs, check_vma=False)
```

profile of v0, /device:TPU:0, one launch (start us, length us, event | category | flops | bytes accessed | tf_op | source)
XLA Modules:
  0.0 409.7 jit_solution(12918442514962170128)
XLA Ops:
  7.2 2.7 copy.16
  10.0 1.1 convert_reduce_fusion.1
  11.2 1.3 fusion.46
  12.5 106.6 %all-gather.2.cloned.1.call-done = bf16[4,1664,416]{2,0,1:T(4,128)(2,1)} async-done(((bf16[4,208,416]{2,0,1:T(4,128)(2,1)}), bf16[4,1664,416]{2,0,1:T(4,128)(2,1)}) %all-gather.2.cloned.1.call-update) | async-done | bytes 5537808 | tf_op jit(solution)/shard_map/all_gather | solution.py:15
  119.0 11.3 %copy.29 = bf16[3,1664,416]{1,2,0:T(8,128)(2,1)} copy(bf16[3,1664,416]{2,0,1:T(4,128)(2,1)} %bitcast.176) | data formatting | bytes 8306688
  130.3 3.5 fusion.33
  134.5 8.4 %slice.30 = bf16[1,1664,416]{2,0,1:T(2,128)(2,1)} slice(bf16[4,1664,416]{2,0,1:T(4,128)(2,1)} %all-gather.2.cloned.1.call-done), slice={[3:4], [0:1664], [0:416]} | slice | bytes 2768896 | tf_op jit(solution)/shard_map/slice | solution.py:34
  142.9 8.5 %copy.30 = bf16[1,1664,416]{1,2,0:T(8,128)(2,1)S(1)} copy(bf16[1,1664,416]{2,0,1:T(2,128)(2,1)} %slice.30) | data formatting | bytes 2768896
  151.5 18.4 %all_gather.7 = bf16[2,512,416]{1,2,0:T(8,128)(2,1)S(1)} all-gather(bf16[2,128,416]{1,2,0:T(8,128)(2,1)} %slice.27), channel_id=1, replica_groups=mesh['grp'=2,'seq'=4,'dp'=2,'pipe'=2] {'seq'}, dimensions={1}, use_global_device_ids=true | all-gather | bytes 1064960 | tf_op jit(solution)/shard_map/all_gather | solution.py:29
  169.9 1.0 fusion.57
  170.9 1.3 copy.19
  172.2 1.3 copy.20
  174.0 16.9 %while.16 = (s32[]{:T(128)}, bf16[4,128,104]{1,2,0:T(8,128)(2,1)}, bf16[4,128,104]{1,2,0:T(8,128)(2,1)}, bf16[4,512,104]{1,2,0:T(8,128)(2,1)}, bf16[4,512,104]{1...) while((s32[]{:T(128)}, bf16[4,128,104]{1,2,0:T(8,128)(2,1)}, ...), condition=%wide.region_6.7_spmd, body=%wide.region_2.6_spmd.sunk | while | flops 82589440 | bytes 2916977 | solution.py:60
  191.0 1.2 pad_maximum_fusion
  192.2 1.0 copy.23
  193.2 1.7 reshape.49
  195.0 1.5 convolution_bitcast_fusion.3
  196.5 21.9 %reduce-scatter.10.cloned.1.call-done = bf16[128,832]{1,0:T(8,128)(2,1)} async-done(((bf16[512,832]{1,0:T(8,128)(2,1)}), bf16[128,832]{1,0:T(8,128)(2,1)}) %reduce-scatter.10.cloned.1.call-update) | async-done | bytes 213008
  218.5 1.9 reshape.50
  220.4 1.1 copy.24
  221.5 1.3 convolution_bitcast_fusion.2
  222.9 3.3 fusion.29
  226.1 11.9 %copy.25 = bf16[4,1664,416]{2,0,1:T(4,128)(2,1)} copy(bf16[4,1664,416]{1,2,0:T(8,128)(2,1)} %fusion.29) | data formatting | bytes 11075584
  238.1 12.9 %reshape.51 = bf16[1664,1664]{1,0:T(8,128)(2,1)} reshape(bf16[1664,4,416]{2,1,0:T(4,128)(2,1)} %bitcast.175) | data formatting | bytes 11075584
  251.0 3.8 fusion.30
  255.1 93.5 %reduce-scatter.12.cloned.1.call-done = bf16[416,1664]{1,0:T(8,128)(2,1)} async-done(((bf16[1664,1664]{1,0:T(8,128)(2,1)}), bf16[416,1664]{1,0:T(8,128)(2,1)}) %reduce-scatter.12.cloned.1.call-update) | async-done | bytes 1384464
  348.6 21.9 %all-reduce.2.cloned.1.call-done = bf16[128,1664]{1,0:T(8,128)(2,1)} async-done(((bf16[128,1664]{1,0:T(8,128)(2,1)}), bf16[128,1664]{1,0:T(8,128)(2,1)}) %all-reduce.2.cloned.1.call-update) | async-done | bytes 426000 | tf_op jit(solution)/shard_map/psum | solution.py:90
  370.5 1.3 convert_reduce_fusion
  371.8 2.2 fusion.48
  374.0 23.8 %reduce-scatter.14.cloned.1.call-done = bf16[208,1664]{1,0:T(8,128)(2,1)} async-done(((bf16[416,1664]{1,0:T(8,128)(2,1)}), bf16[208,1664]{1,0:T(8,128)(2,1)}) %reduce-scatter.14.cloned.1.call-update) | async-done | bytes 692240
  397.8 3.1 reshape.54
  401.7 1.5 copy.22
  (72 shorter events, 19.5 us)
Async XLA Ops:
  7.2 111.9 %all-gather.2.cloned.1.call-start = ((), (), s32[]{:S(2)}) async-start(), calls=%async_computation.3 | async-start | bytes 7667712 | tf_op jit(solution)/shard_map/all_gather | solution.py:15
  10.0 208.5 %reduce-scatter.10.cloned.1.call-start = ((), (), s32[]{:S(2)}) async-start(), calls=%async_computation.5 | async-start | bytes 1146880
  119.0 11.3 %copy-start = (bf16[1,128,1664]{2,1,0:T(8,128)(2,1)S(1)}, bf16[1,128,1664]{2,1,0:T(8,128)(2,1)}, u32[]{:S(2)}) copy-start(bf16[1,128,1664]{2,1,0:T(8,128)(2,1)} %param.5) | copy-start | bytes 1277956
  142.9 30.6 %copy-start.1 = (bf16[1,128,1664]{2,1,0:T(8,128)(2,1)S(1)}, bf16[1,128,1664]{2,1,0:T(8,128)(2,1)}, u32[]{:S(2)}) copy-start(bf16[1,128,1664]{2,1,0:T(8,128)(2,1)} %param.6) | copy-start | bytes 1277956
  191.0 4.0 copy-start.4
  192.2 29.3 %copy-start.3 = (bf16[4,128,104]{1,2,0:T(8,128)(2,1)S(1)}, bf16[4,128,104]{1,2,0:T(8,128)(2,1)}, u32[]{:S(2)}) copy-start(bf16[4,128,104]{1,2,0:T(8,128)(2,1)} %get-tuple-element.52) | copy-start | bytes 319492
  195.0 153.6 %reduce-scatter.12.cloned.1.call-start = ((), (), s32[]{:S(2)}) async-start(), calls=%async_computation.6 | async-start | bytes 6922240
  251.0 120.9 %copy-start.2 = (bf16[1,128,1664]{2,1,0:T(8,128)(2,1)S(1)}, bf16[1,128,1664]{2,1,0:T(8,128)(2,1)}, u32[]{:S(2)}) copy-start(bf16[1,128,1664]{2,1,0:T(8,128)(2,1)} %param.6) | copy-start | bytes 1277956
  251.0 119.5 %all-reduce.2.cloned.1.call-start = ((), (), s32[]{:S(2)}) async-start(), calls=%async_computation.4 | async-start | bytes 851968 | tf_op jit(solution)/shard_map/psum | solution.py:90
  254.8 143.0 %reduce-scatter.14.cloned.1.call-start = ((), (), s32[]{:S(2)}) async-start(), calls=%async_computation.7 | async-start | bytes 2076672
Sparse Core Ops, SparseCore 0:
  10.8 108.2 all-gather.1
  195.1 23.3 reduce-scatter.9
  251.1 97.4 reduce-scatter.11
  351.4 19.0 all-reduce.1
  372.6 25.1 reduce-scatter.13
where the time goes:
time: 411 us; the launch traced here: 410 us
  waiting for transfers between devices  268 us (65%)
  local copies, waits for them, and re-layouts  71.1 us (17%)
  matrix products  26 us (6%)
  blocking collectives  18.4 us (4%)
  between operations  13.9 us (3%)
  other arithmetic  11.9 us (3%)
    unnamed x8, waiting for transfers between devices  139 us
    all_gather x1, waiting for transfers between devices, local(): weights = lax.all_gather(attn_weights, ('seq', 'dp'), axis=1, tiled=True)  107 us
    unnamed x22, local copies, waits for them, and re-layouts  58.4 us
    psum x1, waiting for transfers between devices, local(): lax.psum(input_part.astype(jnp.bfloat16), 'pipe').astype(jnp.float32)  21.9 us
    all_gather x1, blocking collectives, local(): gathered = lax.all_gather(proj[1:], 'seq', axis=1, tiled=True)  18.4 us
    slice x1, local copies, waits for them, and re-layouts, local(): weights[3]  8.39 us
  transfers between devices with their start and end apart: 5, of which 5 were waited for; matrix products, arithmetic and copies ran while one was open for 3% of the time, Pallas kernels for 0%

commit v1 on v0

--- a/solution.py
+++ b/solution.py
@@ -26,7 +26,17 @@
     proj = jnp.einsum(
         "td,cdh->cth", normalized_rows, weights[:3], preferred_element_type=jnp.float32
     ).astype(jnp.bfloat16)
-    gathered = lax.all_gather(proj[1:], "seq", axis=1, tiled=True)
+    value = proj[1:]
+    ways = lax.axis_size("seq")
+    up = [(d, (d + 1) % ways) for d in range(ways)]
+    down = [(d, (d - 1) % ways) for d in range(ways)]
+    earlier, later = ([value], [value])
+    for _ in range(ways // 2):
+        earlier.append(lax.ppermute(earlier[-1], "seq", up))
+    for _ in range((ways - 1) // 2):
+        later.append(lax.ppermute(later[-1], "seq", down))
+    line = jnp.concatenate([*earlier[::-1], *later[1:]], axis=1)
+    gathered = jnp.roll(line, (lax.axis_index("seq") - ways // 2) * value.shape[1], axis=1)
     key_count = gathered.shape[1]
     query_heads = proj[0].reshape(row_count, head_count, HD).transpose(1, 0, 2)
     key_heads = gathered[0].reshape(key_count, head_count, HD).transpose(1, 0, 2)

time: 411 us -> 394 us (0.959)
  blocking collectives: 18.4 us -> 0 us
  waiting for transfers between devices: 268 us -> 276 us
  matrix products: 26 us -> 18.7 us
    all_gather x1 -> x0, blocking collectives: 18.4 us -> none  [local(): gathered = lax.all_gather(proj[1:], 'seq', axis=1, tiled=True)]
    ppermute x0 -> x3, waiting for transfers between devices: none -> 7.27 us  [the longest x2 7.27 us: local(): earlier.append(lax.ppermute(earlier[-1], 'seq', up))]
    unnamed x22 -> x27, local copies, waits for them, and re-layouts: 58.4 us -> 59.2 us
  transfers between devices with their start and end apart: 5 -> 8, of which waited for: 5 -> 6; matrix products, arithmetic and copies ran while one was open for 3% -> 7% of each run, Pallas kernels for 0% -> 0%
where the time goes in v1:
time: 394 us; the launch traced here: 392 us
  waiting for transfers between devices  276 us (70%)
  local copies, waits for them, and re-layouts  69.1 us (18%)
  matrix products  18.7 us (5%)
  between operations  14 us (4%)
  other arithmetic  9.75 us (2%)
  starting transfers between devices  4.32 us (1%)
    unnamed x8, waiting for transfers between devices  138 us
    all_gather x1, waiting for transfers between devices, local(): weights = lax.all_gather(attn_weights, ('seq', 'dp'), axis=1, tiled=True)  109 us
    unnamed x27, local copies, waits for them, and re-layouts  59.2 us
    psum x1, waiting for transfers between devices, local(): lax.psum(input_part.astype(jnp.bfloat16), 'pipe').astype(jnp.float32)  21.9 us
    slice x1, local copies, waits for them, and re-layouts, local(): weights[3]  8.39 us
  transfers between devices with their start and end apart: 8, of which 6 were waited for; matrix products, arithmetic and copies ran while one was open for 7% of the time, Pallas kernels for 0%

profile of v1, /device:TPU:0, one launch (start us, length us, event | category | flops | bytes accessed | tf_op | source)
XLA Modules:
  0.0 392.1 jit_solution(6043234576132205269)
XLA Ops:
  7.2 2.8 copy.16
  10.5 108.6 %all-gather.2.cloned.1.call-done = bf16[4,1664,416]{2,0,1:T(4,128)(2,1)} async-done(((bf16[4,208,416]{2,0,1:T(4,128)(2,1)}), bf16[4,1664,416]{2,0,1:T(4,128)(2,1)}) %all-gather.2.cloned.1.call-update) | async-done | bytes 5537808 | tf_op jit(solution)/shard_map/all_gather | solution.py:15
  119.1 11.2 %copy.29 = bf16[3,1664,416]{1,2,0:T(8,128)(2,1)} copy(bf16[3,1664,416]{2,0,1:T(4,128)(2,1)} %bitcast.176) | data formatting | bytes 8306688
  130.3 3.5 fusion.33
  134.5 3.9 collective-permute-start.2
  138.4 8.4 %slice.28 = bf16[1,1664,416]{2,0,1:T(2,128)(2,1)} slice(bf16[4,1664,416]{2,0,1:T(4,128)(2,1)} %all-gather.2.cloned.1.call-done), slice={[3:4], [0:1664], [0:416]} | slice | bytes 2768896 | tf_op jit(solution)/shard_map/slice | solution.py:44
  146.7 8.5 %copy.30 = bf16[1,1664,416]{1,2,0:T(8,128)(2,1)S(1)} copy(bf16[1,1664,416]{2,0,1:T(2,128)(2,1)} %slice.28) | data formatting | bytes 2768896
  156.0 7.3 %collective-permute-done.1 = bf16[2,128,416]{1,2,0:T(8,128)(2,1)S(1)} collective-permute-done((bf16[2,128,416]{1,2,0:T(8,128)(2,1)S(1)}, bf16[2,128,416]{1,2,0:T(8,128)(2,1)S(1)}, u32[]{:S(2)}, u32[]{:S(2)}) %collective-permute-start.1) | collective-permute-done | bytes 213024 | tf_op jit(solution)/shard_map/ppermute | solution.py:35
  164.9 9.7 %while.16 = (s32[]{:T(128)}, bf16[4,128,104]{1,2,0:T(8,128)(2,1)S(1)}, bf16[4,128,104]{1,2,0:T(8,128)(2,1)S(1)}, bf16[4,512,104]{1,2,0:T(8,128)(2,1)}, bf16[4,51...) while((s32[]{:T(128)}, ...), condition=%wide.region_6.7_spmd, body=%wide.region_2.6_spmd.sunk | while | flops 82589440 | bytes 2916977 | solution.py:70
  166.2 0.9 fusion.90
  168.7 0.9 fusion.90
  171.1 0.9 fusion.90
  173.5 0.9 fusion.90
  174.6 1.1 pad_maximum_fusion
  175.7 1.0 copy.23
  176.6 1.7 reshape.49
  178.4 1.5 convolution_bitcast_fusion.3
  180.0 20.9 %reduce-scatter.10.cloned.1.call-done = bf16[128,832]{1,0:T(8,128)(2,1)} async-done(((bf16[512,832]{1,0:T(8,128)(2,1)}), bf16[128,832]{1,0:T(8,128)(2,1)}) %reduce-scatter.10.cloned.1.call-update) | async-done | bytes 213008
  200.9 1.9 reshape.50
  202.8 1.1 copy.24
  203.9 1.3 convolution_bitcast_fusion.2
  205.2 3.3 fusion.29
  208.5 11.9 %copy.25 = bf16[4,1664,416]{2,0,1:T(4,128)(2,1)} copy(bf16[4,1664,416]{1,2,0:T(8,128)(2,1)} %fusion.29) | data formatting | bytes 11075584
  220.4 12.9 %reshape.51 = bf16[1664,1664]{1,0:T(8,128)(2,1)} reshape(bf16[1664,4,416]{2,1,0:T(4,128)(2,1)} %bitcast.175) | data formatting | bytes 11075584
  233.6 3.7 fusion.30
  237.4 93.6 %reduce-scatter.12.cloned.1.call-done = bf16[416,1664]{1,0:T(8,128)(2,1)} async-done(((bf16[1664,1664]{1,0:T(8,128)(2,1)}), bf16[416,1664]{1,0:T(8,128)(2,1)}) %reduce-scatter.12.cloned.1.call-update) | async-done | bytes 1384464
  331.0 21.9 %all-reduce.2.cloned.1.call-done = bf16[128,1664]{1,0:T(8,128)(2,1)} async-done(((bf16[128,1664]{1,0:T(8,128)(2,1)}), bf16[128,1664]{1,0:T(8,128)(2,1)}) %all-reduce.2.cloned.1.call-update) | async-done | bytes 426000 | tf_op jit(solution)/shard_map/psum | solution.py:100
  352.9 1.3 convert_reduce_fusion
  354.2 2.2 fusion.48
  356.4 23.8 %reduce-scatter.14.cloned.1.call-done = bf16[208,1664]{1,0:T(8,128)(2,1)} async-done(((bf16[416,1664]{1,0:T(8,128)(2,1)}), bf16[208,1664]{1,0:T(8,128)(2,1)}) %reduce-scatter.14.cloned.1.call-update) | async-done | bytes 692240
  380.2 3.1 reshape.54
  384.1 1.5 copy.22
  (83 shorter events, 10.7 us)
Async XLA Ops:
  7.2 2.9 copy-start
  7.2 111.9 %all-gather.2.cloned.1.call-start = ((), (), s32[]{:S(2)}) async-start(), calls=%async_computation.3 | async-start | bytes 7667712 | tf_op jit(solution)/shard_map/all_gather | solution.py:15
  10.0 190.9 %reduce-scatter.10.cloned.1.call-start = ((), (), s32[]{:S(2)}) async-start(), calls=%async_computation.5 | async-start | bytes 1146880
  134.5 20.9 %collective-permute-start = (bf16[2,128,416]{1,2,0:T(8,128)(2,1)}, bf16[2,128,416]{1,2,0:T(8,128)(2,1)S(1)}, u32[]{:S(2)}, u32[]{:S(2)}) collective-permute-start(bf16[2,128,416]{1,2,0:T(8,128)(2,1)} %slice.27), channel_id=1, source_target_pairs={{0,4},{4,8},{8,12},{12,0},{1,5},{5,9},{9,13},{13,1},{2,6},{6,10},{... | collective-permute-start | bytes 638984 | tf_op jit(solution)/shard_map/ppermute | solution.py:35
  134.5 29.0 %collective-permute-start.2 = (bf16[2,128,416]{1,2,0:T(8,128)(2,1)}, bf16[2,128,416]{1,2,0:T(8,128)(2,1)S(1)}, u32[]{:S(2)}, u32[]{:S(2)}) collective-permute-start(bf16[2,128,416]{1,2,0:T(8,128)(2,1)} %slice.27), channel_id=1, source_target_pairs={{0,12},{4,0},{8,4},{12,8},{1,13},{5,1},{9,5},{13,9},{2,14},{6,2},{... | collective-permute-start | bytes 638984 | tf_op jit(solution)/shard_map/ppermute | solution.py:37
  146.7 8.7 %copy-start.1 = (bf16[1,128,1664]{2,1,0:T(8,128)(2,1)S(1)}, bf16[1,128,1664]{2,1,0:T(8,128)(2,1)}, u32[]{:S(2)}) copy-start(bf16[1,128,1664]{2,1,0:T(8,128)(2,1)} %param.6) | copy-start | bytes 1277956
  155.4 7.9 %collective-permute-start.1 = (bf16[2,128,416]{1,2,0:T(8,128)(2,1)S(1)}, bf16[2,128,416]{1,2,0:T(8,128)(2,1)S(1)}, u32[]{:S(2)}, u32[]{:S(2)}) collective-permute-start(bf16[2,128,416]{1,2,0:T(8,128)(2,1)S(1)} %collective-permute-done), channel_id=1, source_target_pairs={{0,4},{4,8},{8,12},{12,0},{1,5},{5,9},{9,13},{13,1},{2,6},{6,10},{... | collective-permute-start | bytes 638984 | tf_op jit(solution)/shard_map/ppermute | solution.py:35
  163.9 1.0 copy-start.3
  178.4 152.6 %reduce-scatter.12.cloned.1.call-start = ((), (), s32[]{:S(2)}) async-start(), calls=%async_computation.6 | async-start | bytes 6922240
  233.4 119.5 %all-reduce.2.cloned.1.call-start = ((), (), s32[]{:S(2)}) async-start(), calls=%async_computation.4 | async-start | bytes 851968 | tf_op jit(solution)/shard_map/psum | solution.py:100
  237.3 116.9 %copy-start.2 = (bf16[1,128,1664]{2,1,0:T(8,128)(2,1)S(1)}, bf16[1,128,1664]{2,1,0:T(8,128)(2,1)}, u32[]{:S(2)}) copy-start(bf16[1,128,1664]{2,1,0:T(8,128)(2,1)} %param.6) | copy-start | bytes 1277956
  237.3 142.8 %reduce-scatter.14.cloned.1.call-start = ((), (), s32[]{:S(2)}) async-start(), calls=%async_computation.7 | async-start | bytes 2076672
Sparse Core Ops, SparseCore 0:
  10.8 108.2 all-gather.1
  178.5 22.3 reduce-scatter.9
  233.5 97.4 reduce-scatter.11
  333.7 19.0 all-reduce.1
  355.0 25.1 reduce-scatter.13
